TPU v7x, 128 devices: a whole 4x4x4 slice. The times are simulated.
128 devices in a mesh: dp: 16 (over y, z), mp: 8 (over x, core).
Axes of the slice: x: 4, y: 4, z: 4, core: 2. Of those that a mesh axis runs over, the one named last changes fastest.
Arguments:
- grad_out: bfloat16 [16384, 6144], P(('dp', 'mp')), may hold values from -40 to 40
- context: bfloat16 [16384, 6144], P('dp', 'mp'), may hold values from -47 to 47
- weight: bfloat16 [6144, 6144], P(None, 'mp'), may hold values from -0.078125 to 0.078125
- master: float32 [6144, 6144], P('dp', 'mp'), may hold values from -0.6 to 0.6
- moment_q: bfloat16 [6144, 6144], P('dp', 'mp'), may hold values from -440 to 440
- second_moment: float32 [6144, 6144], P('dp', 'mp'), may hold values from 0.02 to 1
- moment_scale: float32 [], replicated, may hold values from 300 to 900
- scale_boost: float32 [], replicated, may hold values from 1.25 to 2
Outputs:
- input_grad: bfloat16 [16384, 6144], P('dp', 'mp')
- new_master: float32 [6144, 6144], P('dp', 'mp')
- new_moment_q: bfloat16 [6144, 6144], P('dp', 'mp')
- new_second: float32 [6144, 6144], P('dp', 'mp')
- new_scale: float32 [], replicated
- grad_scale: float32 [], replicated
- new_weight: bfloat16 [6144, 6144], P(None, 'mp')
All inputs are finite; a program needn't handle non-finite values. Where the computation divides by a largest or mean magnitude, that divisor is 1e-20 or more.
Results may differ from a plain program's by a relative error of at most 0.014.
Values may be sent and summed in bfloat16 or wider, within the bound.
No kernel may reach another device: no remote copies, remote signals or barrier semaphores. Data moves between devices by JAX's collectives and lax.ppermute only.
A program may use at most 128 MiB of HBM per device.

v0:
```python
import math
import jax
import jax.numpy as jnp
from jax import lax
from jax.sharding import PartitionSpec as P

D = 6144
HD = 6144
N_DEV = 128
LANES = 128
quant_top = 448.0
peak_eps = 1e-06
norm_eps = 1e-06
clip_rms = 0.5
beta_one = 0.9
beta_two = 0.95
bias_one = 1.0 - 0.9**10
bias_two = 1.0 - 0.95**10
adam_eps = 1e-08
rate_value = 0.01
decay_value = 0.1
contract_rows = (((0,), (0,)), ((), ()))


def input_product(full_grad, weight):
    return jnp.dot(full_grad, weight, preferred_element_type=jnp.float32).astype(jnp.bfloat16)


def spread(value):
    rows = jnp.broadcast_to(value, (N_DEV, LANES))
    return lax.all_to_all(rows, ("dp", "mp"), 0, 0, tiled=True)


def global_max(value):
    return jnp.max(spread(value))


def global_sum(value):
    return jnp.sum(spread(value)[:, 0])


def weight_gradient(full_grad, context, scale_boost):
    held = lax.dot_general(full_grad, context, contract_rows, preferred_element_type=jnp.float32)
    local_peak = jnp.max(jnp.abs(held))
    peak = global_max(local_peak)
    grad_scale = quant_top * scale_boost / (peak + peak_eps)
    scaled = held * grad_scale
    summed = lax.psum_scatter(
        jnp.clip(scaled, -quant_top, quant_top).astype(jnp.bfloat16),
        "dp",
        scatter_dimension=0,
        tiled=True,
    ).astype(jnp.float32)
    return (summed, grad_scale)


def local(grad_out, context, weight, master, moment_q, second_moment, moment_scale, scale_boost):
    full_grad = lax.all_gather(grad_out, "mp", axis=0, tiled=True)
    input_grad = input_product(full_grad, weight)
    summed, grad_scale = weight_gradient(full_grad, context, scale_boost)
    gradient = summed / grad_scale
    squares = global_sum(jnp.sum(gradient * gradient))
    norm_value = jnp.sqrt(squares + norm_eps)
    clip_factor = clip_rms * math.sqrt(D * HD) / norm_value
    step_grad = clip_factor * gradient
    old_moment = moment_q.astype(jnp.float32) / moment_scale
    moment = beta_one * old_moment + (1.0 - beta_one) * step_grad
    new_second = beta_two * second_moment + (1.0 - beta_two) * step_grad * step_grad
    update = moment / bias_one / (jnp.sqrt(new_second / bias_two) + adam_eps) + decay_value * master
    new_master = master - rate_value * update
    moment_top = global_max(jnp.max(jnp.abs(moment)))
    new_scale = quant_top / (moment_top + peak_eps)
    new_moment_q = (moment * new_scale).astype(jnp.bfloat16)
    new_weight = lax.all_gather(new_master.astype(jnp.bfloat16), "dp", axis=0, tiled=True)
    return (input_grad, new_master, new_moment_q, new_second, new_scale, grad_scale, new_weight)


def solution(mesh):
    return jax.shard_map(
        local,
        mesh=mesh,
        in_specs=(
            P(("dp", "mp"), None),
            P("dp", "mp"),
            P(None, "mp"),
            P("dp", "mp"),
            P("dp", "mp"),
            P("dp", "mp"),
            P(),
            P(),
        ),
        out_specs=(
            P("dp", "mp"),
            P("dp", "mp"),
            P("dp", "mp"),
            P("dp", "mp"),
            P(),
            P(),
            P(None, "mp"),
        ),
        check_vma=False,
    )
```

profile of v0, /device:TPU:1, one launch (start us, length us, event | category | flops | bytes accessed | tf_op | source)
XLA Modules:
  0.0 329.5 jit_solution(7558855803893621168)
XLA Ops:
  7.2 0.0 copy-start
  7.2 0.0 all-gather.3.cloned.1.call-start
  7.2 0.7 all-gather.3.cloned.1.call-update
  7.9 72.8 %all-gather.3.cloned.1.call-done = bf16[1024,6144]{1,0:T(8,128)(2,1)} async-done(((bf16[128,6144]{1,0:T(8,128)(2,1)}), bf16[1024,6144]{1,0:T(8,128)(2,1)}) %all-gather.3.cloned.1.call-update) | async-done | bytes 12582928 | tf_op jit(solution)/shard_map/all_gather | solution.py:58
  80.7 0.0 copy-done
  80.7 17.7 %abs_reduce_fusion = (f32[]{:T(128)}, f32[6144,768]{1,0:T(8,128)}) fusion(bf16[1024,6144]{1,0:T(8,128)(2,1)} %all-gather.3.cloned.1.call-done, bf16[1024,768]{1,0:T(8,128)(2,1)S(1)} %copy-done), kind=kOutput, calls=%fused_computation.1 | convolution fusion | flops 9673113600 | bytes 33030148 | tf_op jit(solution)/shard_map/dot_general | solution.py:43
  98.3 1.3 broadcast_in_dim.9
  99.6 8.3 %all-to-all-start = ((f32[128,1,128]{2,1,0:T(1,128)}), f32[128,1,128]{2,1,0:T(1,128)S(1)}, u32[]{:S(2)}, u32[]{:S(2)}) async-start(f32[128,1,128]{2,1,0:T(1,128)} %broadcast_in_dim.9), calls=%async_computation | async-start | bytes 131072 | tf_op jit(solution)/shard_map/all_to_all | solution.py:31
  107.9 0.0 reduce-scatter.2.cloned.1.call-start
  108.6 8.7 %all-to-all-done = f32[128,1,128]{2,1,0:T(1,128)S(1)} async-done(((f32[128,1,128]{2,1,0:T(1,128)}), f32[128,1,128]{2,1,0:T(1,128)S(1)}, u32[]{:S(2)}, u32[]{:S(2)}) %all-to-all-start) | async-done | bytes 65568 | tf_op jit(solution)/shard_map/all_to_all | solution.py:31
  117.3 0.6 reduce_max.37
  118.6 11.6 %clamp_convert_fusion = bf16[6144,768]{1,0:T(8,128)(2,1)} fusion(f32[6144,768]{1,0:T(8,128)} %get-tuple-element.12, f32[]{:T(128)} %div.38), kind=kLoop, calls=%fused_computation | loop fusion | flops 14155776 | bytes 28311556 | tf_op jit(solution)/shard_map/convert_element_type | solution.py:49
  130.2 0.0 copy-start.3
  130.2 0.0 reduce-scatter.2.cloned.1.call-update
  130.2 83.3 %reduce-scatter.2.cloned.1.call-done = bf16[384,768]{1,0:T(8,128)(2,1)} async-done(((bf16[6144,768]{1,0:T(8,128)(2,1)}), bf16[384,768]{1,0:T(8,128)(2,1)}) %reduce-scatter.2.cloned.1.call-update) | async-done | bytes 589840 | tf_op jit(solution)/shard_map/reduce_scatter | solution.py:48
  213.5 0.0 copy-start.2
  213.5 2.0 multiply_reduce_fusion
  215.5 1.3 broadcast_in_dim.10
  216.8 8.3 %all-to-all-start.1 = ((f32[128,1,128]{2,1,0:T(1,128)}), f32[128,1,128]{2,1,0:T(1,128)S(1)}, u32[]{:S(2)}, u32[]{:S(2)}) async-start(f32[128,1,128]{2,1,0:T(1,128)} %broadcast_in_dim.10), calls=%async_computation.2 | async-start | bytes 131072 | tf_op jit(solution)/shard_map/all_to_all | solution.py:31
  225.1 0.0 all-gather.5.cloned.1.call-start
  225.8 8.7 %all-to-all-done.1 = f32[128,1,128]{2,1,0:T(1,128)S(1)} async-done(((f32[128,1,128]{2,1,0:T(1,128)}), f32[128,1,128]{2,1,0:T(1,128)S(1)}, u32[]{:S(2)}, u32[]{:S(2)}) %all-to-all-start.1) | async-done | bytes 65568 | tf_op jit(solution)/shard_map/all_to_all | solution.py:31
  234.5 0.6 slice_reduce_fusion
  235.9 0.0 copy-done.3
  235.9 0.0 copy-done.2
  235.9 4.1 %fusion.1 = (bf16[384,768]{1,0:T(8,128)(2,1)}, f32[384,768]{1,0:T(8,128)}, f32[384,768]{1,0:T(8,128)S(1)}, f32[384,768]{1,0:T(8,128)}) fusion(f32[384,768]{1,0:T(8,128)S(1)} %copy-done.3, f32[]{:T(128)} %div.38, bf16[384,768]{1,0:T(8,128)(2,1)S(1)} %copy-done.2, f32[]{:T(128)S(6)} %div.41, f32[]{:T(128)S(6)} %copy.20, bf16[384,768]{1,0:T(8,128)(2,1)} %param.12, ...), kind=kLoop, calls=%fused_computation.12 | loop fusion | flops 6193152 | bytes 7667724 | tf_op jit(solution)/shard_map/convert_element_type | solution.py:74
  240.0 0.0 all-gather.5.cloned.1.call-update
  240.0 0.7 abs_reduce_fusion.1
  240.7 1.3 broadcast_in_dim.11
  242.0 4.6 %all-to-all-start.2 = ((f32[128,1,128]{2,1,0:T(1,128)}), f32[128,1,128]{2,1,0:T(1,128)S(1)}, u32[]{:S(2)}, u32[]{:S(2)}) async-start(f32[128,1,128]{2,1,0:T(1,128)} %broadcast_in_dim.11), calls=%async_computation.3 | async-start | bytes 131072 | tf_op jit(solution)/shard_map/all_to_all | solution.py:31
  246.6 15.8 %convolution_convert_fusion = bf16[1024,768]{1,0:T(8,128)(2,1)} fusion(bf16[1024,6144]{1,0:T(8,128)(2,1)} %all-gather.3.cloned.1.call-done, bf16[6144,768]{1,0:T(8,128)(2,1)} %param.10), kind=kOutput, calls=%fused_computation.3 | convolution fusion | flops 9664462848 | bytes 23592960 | tf_op jit(solution)/shard_map/dot_general | solution.py:26
  262.5 0.0 all-to-all-done.2
  262.5 0.6 reduce_max.39
  263.8 0.9 multiply_convert_fusion
  264.7 48.0 %all-gather.5.cloned.1.call-done = bf16[6144,768]{1,0:T(8,128)(2,1)} async-done(((bf16[384,768]{1,0:T(8,128)(2,1)}), bf16[6144,768]{1,0:T(8,128)(2,1)}) %all-gather.5.cloned.1.call-update) | async-done | bytes 9437200 | tf_op jit(solution)/shard_map/all_gather | solution.py:74
  312.6 0.0 copy-start.1
  312.6 8.1 %copy.22 = bf16[6144,768]{1,0:T(8,128)(2,1)} copy(bf16[6144,768]{1,0:T(8,128)(2,1)} %all-gather.5.cloned.1.call-done) | data formatting | bytes 18874368
  320.8 0.0 copy-done.1
Async XLA Ops:
  7.2 73.5 %copy-start = (bf16[1024,768]{1,0:T(8,128)(2,1)S(1)}, bf16[1024,768]{1,0:T(8,128)(2,1)}, u32[]{:S(2)}) copy-start(bf16[1024,768]{1,0:T(8,128)(2,1)} %param.9) | copy-start | bytes 4718596
  7.2 73.5 %all-gather.3.cloned.1.call-start = ((), (), s32[]{:S(2)}) async-start(), calls=%async_computation.4 | async-start | bytes 14155776 | tf_op jit(solution)/shard_map/all_gather | solution.py:58
  99.6 17.7 %all-to-all-start = ((f32[128,1,128]{2,1,0:T(1,128)}), f32[128,1,128]{2,1,0:T(1,128)S(1)}, u32[]{:S(2)}, u32[]{:S(2)}) async-start(f32[128,1,128]{2,1,0:T(1,128)} %broadcast_in_dim.9), calls=%async_computation | async-start | bytes 131072 | tf_op jit(solution)/shard_map/all_to_all | solution.py:31
  107.9 105.6 %reduce-scatter.2.cloned.1.call-start = ((), (), s32[]{:S(2)}) async-start(), calls=%async_computation.5 | async-start | bytes 10027008 | tf_op jit(solution)/shard_map/reduce_scatter | solution.py:48
  130.2 105.7 %copy-start.3 = (f32[384,768]{1,0:T(8,128)S(1)}, f32[384,768]{1,0:T(8,128)}, u32[]{:S(2)}) copy-start(f32[384,768]{1,0:T(8,128)} %param.11) | copy-start | bytes 3538948
  213.5 22.4 %copy-start.2 = (bf16[384,768]{1,0:T(8,128)(2,1)S(1)}, bf16[384,768]{1,0:T(8,128)(2,1)}, u32[]{:S(2)}) copy-start(bf16[384,768]{1,0:T(8,128)(2,1)} %reduce-scatter.2.cloned.1.call-done) | copy-start | bytes 1769476
  216.8 17.7 %all-to-all-start.1 = ((f32[128,1,128]{2,1,0:T(1,128)}), f32[128,1,128]{2,1,0:T(1,128)S(1)}, u32[]{:S(2)}, u32[]{:S(2)}) async-start(f32[128,1,128]{2,1,0:T(1,128)} %broadcast_in_dim.10), calls=%async_computation.2 | async-start | bytes 131072 | tf_op jit(solution)/shard_map/all_to_all | solution.py:31
  225.1 87.5 %all-gather.5.cloned.1.call-start = ((), (), s32[]{:S(2)}) async-start(), calls=%async_computation.6 | async-start | bytes 10027008 | tf_op jit(solution)/shard_map/all_gather | solution.py:74
  242.0 20.4 %all-to-all-start.2 = ((f32[128,1,128]{2,1,0:T(1,128)}), f32[128,1,128]{2,1,0:T(1,128)S(1)}, u32[]{:S(2)}, u32[]{:S(2)}) async-start(f32[128,1,128]{2,1,0:T(1,128)} %broadcast_in_dim.11), calls=%async_computation.3 | async-start | bytes 131072 | tf_op jit(solution)/shard_map/all_to_all | solution.py:31
  312.6 8.2 %copy-start.1 = (bf16[1024,768]{1,0:T(8,128)(2,1)S(1)}, bf16[1024,768]{1,0:T(8,128)(2,1)}, u32[]{:S(2)}) copy-start(bf16[1024,768]{1,0:T(8,128)(2,1)} %param.9) | copy-start | bytes 4718596
Sparse Core Ops, SparseCore 0:
  9.7 70.9 all-gather.2
  130.3 83.0 reduce-scatter.1
  240.1 72.4 all-gather.4
where the time goes:
time: 330 us
  waiting for transfers between devices  222 us (67%)
  matrix products  33.5 us (10%)
  starting transfers between devices  21.3 us (6%)
  other arithmetic  21.1 us (6%)
  between operations  19.4 us (6%)
  local copies, waits for them, and re-layouts  12.1 us (4%)
    reduce_scatter x1, waiting for transfers between devices, weight_gradient(): lax.psum_scatter(jnp.clip(scaled, -quant_top, quant_top).astype(jnp.bfloa...  83.3 us
    all_gather x1, waiting for transfers between devices, local(): full_grad = lax.all_gather(grad_out, 'mp', axis=0, tiled=True)  72.8 us
    all_gather x1, waiting for transfers between devices, local(): lax.all_gather(new_master.astype(jnp.bfloat16), 'dp', axis=0, tiled=True)  48 us
    all_to_all x3, starting transfers between devices, spread(): return lax.all_to_all(rows, ('dp', 'mp'), 0, 0, tiled=True)  21.1 us
    dot_general x1, matrix products, weight_gradient(): lax.dot_general(full_grad, context, contract_rows, preferred_element_type...  17.7 us
    all_to_all x3, waiting for transfers between devices, spread(): return lax.all_to_all(rows, ('dp', 'mp'), 0, 0, tiled=True)  17.5 us
    dot_general x1, matrix products, input_product(): jnp.dot(full_grad, weight, preferred_element_type=jnp.float32)  15.8 us
    convert_element_type x1, other arithmetic, weight_gradient(): jnp.clip(scaled, -quant_top, quant_top).astype(jnp.bfloat16)  11.6 us
  transfers between devices with their start and end apart: 6, of which 5 were waited for; matrix products, arithmetic and copies ran while one was open for 6% of the time, Pallas kernels for 0%

commit v1 on v0

--- a/solution.py
+++ b/solution.py
@@ -20,6 +20,11 @@
 rate_value = 0.01
 decay_value = 0.1
 contract_rows = (((0,), (0,)), ((), ()))
+
+
+def all_by_exchange(value, axis, d):
+    outgoing = jnp.stack([value] * lax.axis_size(axis))
+    return jnp.concatenate(lax.all_to_all(outgoing, axis, 0, 0), axis=d)
 
 
 def input_product(full_grad, weight):
@@ -71,7 +76,7 @@
     moment_top = global_max(jnp.max(jnp.abs(moment)))
     new_scale = quant_top / (moment_top + peak_eps)
     new_moment_q = (moment * new_scale).astype(jnp.bfloat16)
-    new_weight = lax.all_gather(new_master.astype(jnp.bfloat16), "dp", axis=0, tiled=True)
+    new_weight = all_by_exchange(new_master.astype(jnp.bfloat16), "dp", 0)
     return (input_grad, new_master, new_moment_q, new_second, new_scale, grad_scale, new_weight)
 
 

time: 330 us -> 451 us (1.37); the launches traced: 330 us -> 442 us
  waiting for transfers between devices: 222 us -> 317 us
  blocking collectives: 0 us -> 13.9 us
    all_to_all x0 -> x1, waiting for transfers between devices: none -> 143 us  [all_by_exchange(): return jnp.concatenate(lax.all_to_all(outgoing, axis, 0, 0), axis=d)]
    all_gather x1 -> x0, waiting for transfers between devices: 48 us -> none  [local(): lax.all_gather(new_master.astype(jnp.bfloat16), 'dp', axis=0, tiled=True)]
    all_to_all x0 -> x1, blocking collectives: none -> 13.9 us  [spread(): return lax.all_to_all(rows, ('dp', 'mp'), 0, 0, tiled=True)]
    all_to_all x0 -> x1, starting transfers between devices: none -> 4.96 us  [all_by_exchange(): return jnp.concatenate(lax.all_to_all(outgoing, axis, 0, 0), axis=d)]
    another operation x0 -> x1, local copies, waits for them, and re-layouts: none -> 4.66 us  [all_by_exchange(): outgoing = jnp.stack([value] * lax.axis_size(axis))]
    all_to_all x3 -> x2, starting transfers between devices: 21.1 us -> 16.5 us  [spread(): return lax.all_to_all(rows, ('dp', 'mp'), 0, 0, tiled=True)]
    all_to_all x3 -> x2, waiting for transfers between devices: 17.5 us -> 17.5 us  [spread(): return lax.all_to_all(rows, ('dp', 'mp'), 0, 0, tiled=True)]
  transfers between devices with their start and end apart: 6 -> 5, of which waited for: 5 -> 5; matrix products, arithmetic and copies ran while one was open for 6% -> 4% of each run, Pallas kernels for 0% -> 0%
where the time goes in v1:
time: 451 us; the launch traced here: 442 us
  waiting for transfers between devices  317 us (70%)
  matrix products  33.3 us (7%)
  starting transfers between devices  21.6 us (5%)
  other arithmetic  20.9 us (5%)
  between operations  19.7 us (4%)
  local copies, waits for them, and re-layouts  16.1 us (4%)
  blocking collectives  13.9 us (3%)
    all_to_all x1, waiting for transfers between devices, all_by_exchange(): return jnp.concatenate(lax.all_to_all(outgoing, axis, 0, 0), axis=d)  143 us
    reduce_scatter x1, waiting for transfers between devices, weight_gradient(): lax.psum_scatter(jnp.clip(scaled, -quant_top, quant_top).astype(jnp.bfloa...  83.3 us
    all_gather x1, waiting for transfers between devices, local(): full_grad = lax.all_gather(grad_out, 'mp', axis=0, tiled=True)  72.8 us
    dot_general x1, matrix products, weight_gradient(): lax.dot_general(full_grad, context, contract_rows, preferred_element_type...  17.7 us
    all_to_all x2, waiting for transfers between devices, spread(): return lax.all_to_all(rows, ('dp', 'mp'), 0, 0, tiled=True)  17.5 us
    all_to_all x2, starting transfers between devices, spread(): return lax.all_to_all(rows, ('dp', 'mp'), 0, 0, tiled=True)  16.5 us
    dot_general x1, matrix products, input_product(): jnp.dot(full_grad, weight, preferred_element_type=jnp.float32)  15.6 us
    all_to_all x1, blocking collectives, spread(): return lax.all_to_all(rows, ('dp', 'mp'), 0, 0, tiled=True)  13.9 us
  transfers between devices with their start and end apart: 5, of which 5 were waited for; matrix products, arithmetic and copies ran while one was open for 4% of the time, Pallas kernels for 0%

profile of v1, /device:TPU:1, one launch (start us, length us, event | category | flops | bytes accessed | tf_op | source)
XLA Modules:
  0.0 442.4 jit_solution(1396687038744124058)
XLA Ops:
  7.2 0.0 copy-start
  7.2 0.0 all-gather.2.cloned.1.call-start
  7.2 0.7 all-gather.2.cloned.1.call-update
  7.9 72.8 %all-gather.2.cloned.1.call-done = bf16[1024,6144]{1,0:T(8,128)(2,1)} async-done(((bf16[128,6144]{1,0:T(8,128)(2,1)}), bf16[1024,6144]{1,0:T(8,128)(2,1)}) %all-gather.2.cloned.1.call-update) | async-done | bytes 12582928 | tf_op jit(solution)/shard_map/all_gather | solution.py:63
  80.7 0.0 copy-done
  80.7 17.7 %abs_reduce_fusion = (f32[]{:T(128)}, f32[6144,768]{1,0:T(8,128)}) fusion(bf16[1024,6144]{1,0:T(8,128)(2,1)} %all-gather.2.cloned.1.call-done, bf16[1024,768]{1,0:T(8,128)(2,1)S(1)} %copy-done), kind=kOutput, calls=%fused_computation.1 | convolution fusion | flops 9673113600 | bytes 33030148 | tf_op jit(solution)/shard_map/dot_general | solution.py:48
  98.3 1.3 broadcast_in_dim.9
  99.6 8.3 %all-to-all-start = ((f32[128,1,128]{2,1,0:T(1,128)}), f32[128,1,128]{2,1,0:T(1,128)S(1)}, u32[]{:S(2)}, u32[]{:S(2)}) async-start(f32[128,1,128]{2,1,0:T(1,128)} %broadcast_in_dim.9), calls=%async_computation | async-start | bytes 131072 | tf_op jit(solution)/shard_map/all_to_all | solution.py:36
  107.9 0.0 reduce-scatter.2.cloned.1.call-start
  108.6 8.7 %all-to-all-done = f32[128,1,128]{2,1,0:T(1,128)S(1)} async-done(((f32[128,1,128]{2,1,0:T(1,128)}), f32[128,1,128]{2,1,0:T(1,128)S(1)}, u32[]{:S(2)}, u32[]{:S(2)}) %all-to-all-start) | async-done | bytes 65568 | tf_op jit(solution)/shard_map/all_to_all | solution.py:36
  117.3 0.6 reduce_max.37
  118.6 11.6 %clamp_convert_fusion = bf16[6144,768]{1,0:T(8,128)(2,1)} fusion(f32[6144,768]{1,0:T(8,128)} %get-tuple-element.12, f32[]{:T(128)} %div.38), kind=kLoop, calls=%fused_computation | loop fusion | flops 14155776 | bytes 28311556 | tf_op jit(solution)/shard_map/convert_element_type | solution.py:54
  130.2 0.0 copy-start.3
  130.2 0.0 reduce-scatter.2.cloned.1.call-update
  130.2 83.3 %reduce-scatter.2.cloned.1.call-done = bf16[384,768]{1,0:T(8,128)(2,1)} async-done(((bf16[6144,768]{1,0:T(8,128)(2,1)}), bf16[384,768]{1,0:T(8,128)(2,1)}) %reduce-scatter.2.cloned.1.call-update) | async-done | bytes 589840 | tf_op jit(solution)/shard_map/reduce_scatter | solution.py:53
  213.5 0.0 copy-start.2
  213.5 2.0 multiply_reduce_fusion
  215.5 1.3 broadcast_in_dim.10
  216.8 8.3 %all-to-all-start.1 = ((f32[128,1,128]{2,1,0:T(1,128)}), f32[128,1,128]{2,1,0:T(1,128)S(1)}, u32[]{:S(2)}, u32[]{:S(2)}) async-start(f32[128,1,128]{2,1,0:T(1,128)} %broadcast_in_dim.10), calls=%async_computation.2 | async-start | bytes 131072 | tf_op jit(solution)/shard_map/all_to_all | solution.py:36
  225.8 8.8 %all-to-all-done.1 = f32[128,1,128]{2,1,0:T(1,128)S(1)} async-done(((f32[128,1,128]{2,1,0:T(1,128)}), f32[128,1,128]{2,1,0:T(1,128)S(1)}, u32[]{:S(2)}, u32[]{:S(2)}) %all-to-all-start.1) | async-done | bytes 65568 | tf_op jit(solution)/shard_map/all_to_all | solution.py:36
  234.5 0.6 slice_reduce_fusion
  235.9 0.0 copy-done.3
  235.9 0.0 copy-done.2
  235.9 3.9 fusion.1
  239.8 0.7 abs_reduce_fusion.1
  240.5 0.7 broadcast_in_dim.11
  241.2 13.9 %all_to_all.26 = f32[128,1,128]{2,1,0:T(1,128)S(1)} all-to-all(f32[128,1,128]{2,1,0:T(1,128)S(1)} %broadcast_in_dim.11), channel_id=1, replica_groups=mesh['dp'=16,'mp'=8] {'dp','mp'}, dimensions={0} | all-to-all | bytes 131072 | tf_op jit(solution)/shard_map/all_to_all | solution.py:36
  255.1 4.7 %stack.2 = bf16[16,384,768]{2,1,0:T(8,128)(2,1)} broadcast(bf16[384,768]{1,0:T(8,128)(2,1)S(1)} %get-tuple-element.7), dimensions={1,2} | broadcast | bytes 10027008 | tf_op jit(solution)/shard_map/stack | solution.py:26
  259.7 5.0 %all-to-all-start.3 = ((bf16[16,384,768]{2,1,0:T(8,128)(2,1)}), bf16[16,384,768]{2,1,0:T(8,128)(2,1)}, u32[]{:S(2)}, u32[]{:S(2)}) async-start(bf16[16,384,768]{2,1,0:T(8,128)(2,1)} %stack.2), calls=%async_computation.4 | async-start | bytes 18874368 | tf_op jit(solution)/shard_map/all_to_all | solution.py:27
  264.7 15.6 %convolution_convert_fusion = bf16[1024,768]{1,0:T(8,128)(2,1)} fusion(bf16[1024,6144]{1,0:T(8,128)(2,1)} %all-gather.2.cloned.1.call-done, bf16[6144,768]{1,0:T(8,128)(2,1)} %param.10), kind=kOutput, calls=%fused_computation.3 | convolution fusion | flops 9664462848 | bytes 23592960 | tf_op jit(solution)/shard_map/dot_general | solution.py:31
  280.4 0.6 reduce_max.39
  281.7 0.9 multiply_convert_fusion
  282.6 142.6 %all-to-all-done.3 = bf16[16,384,768]{2,1,0:T(8,128)(2,1)} async-done(((bf16[16,384,768]{2,1,0:T(8,128)(2,1)}), bf16[16,384,768]{2,1,0:T(8,128)(2,1)}, u32[]{:S(2)}, u32[]{:S(2)}) %all-to-all-start.3) | async-done | bytes 9437216 | tf_op jit(solution)/shard_map/all_to_all | solution.py:27
  425.2 0.0 copy-start.1
  425.2 8.1 %copy.22 = bf16[6144,768]{1,0:T(8,128)(2,1)} copy(bf16[6144,768]{1,0:T(8,128)(2,1)} %bitcast.3) | data formatting | bytes 18874368
  433.3 0.0 copy-done.1
Async XLA Ops:
  7.2 73.5 %copy-start = (bf16[1024,768]{1,0:T(8,128)(2,1)S(1)}, bf16[1024,768]{1,0:T(8,128)(2,1)}, u32[]{:S(2)}) copy-start(bf16[1024,768]{1,0:T(8,128)(2,1)} %param.9) | copy-start | bytes 4718596
  7.2 73.5 %all-gather.2.cloned.1.call-start = ((), (), s32[]{:S(2)}) async-start(), calls=%async_computation.5 | async-start | bytes 14155776 | tf_op jit(solution)/shard_map/all_gather | solution.py:63
  99.6 17.7 %all-to-all-start = ((f32[128,1,128]{2,1,0:T(1,128)}), f32[128,1,128]{2,1,0:T(1,128)S(1)}, u32[]{:S(2)}, u32[]{:S(2)}) async-start(f32[128,1,128]{2,1,0:T(1,128)} %broadcast_in_dim.9), calls=%async_computation | async-start | bytes 131072 | tf_op jit(solution)/shard_map/all_to_all | solution.py:36
  107.9 105.6 %reduce-scatter.2.cloned.1.call-start = ((), (), s32[]{:S(2)}) async-start(), calls=%async_computation.6 | async-start | bytes 10027008 | tf_op jit(solution)/shard_map/reduce_scatter | solution.py:53
  130.2 105.7 %copy-start.3 = (f32[384,768]{1,0:T(8,128)S(1)}, f32[384,768]{1,0:T(8,128)}, u32[]{:S(2)}) copy-start(f32[384,768]{1,0:T(8,128)} %param.11) | copy-start | bytes 3538948
  213.5 22.4 %copy-start.2 = (bf16[384,768]{1,0:T(8,128)(2,1)S(1)}, bf16[384,768]{1,0:T(8,128)(2,1)}, u32[]{:S(2)}) copy-start(bf16[384,768]{1,0:T(8,128)(2,1)} %reduce-scatter.2.cloned.1.call-done) | copy-start | bytes 1769476
  216.8 17.7 %all-to-all-start.1 = ((f32[128,1,128]{2,1,0:T(1,128)}), f32[128,1,128]{2,1,0:T(1,128)S(1)}, u32[]{:S(2)}, u32[]{:S(2)}) async-start(f32[128,1,128]{2,1,0:T(1,128)} %broadcast_in_dim.10), calls=%async_computation.2 | async-start | bytes 131072 | tf_op jit(solution)/shard_map/all_to_all | solution.py:36
  259.7 165.4 %all-to-all-start.3 = ((bf16[16,384,768]{2,1,0:T(8,128)(2,1)}), bf16[16,384,768]{2,1,0:T(8,128)(2,1)}, u32[]{:S(2)}, u32[]{:S(2)}) async-start(bf16[16,384,768]{2,1,0:T(8,128)(2,1)} %stack.2), calls=%async_computation.4 | async-start | bytes 18874368 | tf_op jit(solution)/shard_map/all_to_all | solution.py:27
  425.2 8.2 %copy-start.1 = (bf16[1024,768]{1,0:T(8,128)(2,1)S(1)}, bf16[1024,768]{1,0:T(8,128)(2,1)}, u32[]{:S(2)}) copy-start(bf16[1024,768]{1,0:T(8,128)(2,1)} %param.9) | copy-start | bytes 4718596
Sparse Core Ops, SparseCore 0:
  9.7 70.9 all-gather.1
  130.3 83.0 reduce-scatter.1
